TPU v7x, 256 devices: a whole 4x4x8 slice. The times are simulated.
256 devices in a mesh: row: 32 (over z, y_lo, core), col: 8 (over y_hi, x).
Axes of the slice: x: 4, y: 4 (y_hi: 2, y_lo: 2; y = y_hi * 2 + y_lo), z: 8, core: 2. Of those that a mesh axis runs over, the one named last changes fastest.
Arguments:
- coupling: bfloat16 [16384, 4096], P('row', 'col'), may hold values from 0.19921875 to 5
- source_dist: bfloat16 [16384, 16384], P('row'), may hold values from -0.013531647 to 0.013531647, as said below
- target_dist: bfloat16 [4096, 4096], P('row', 'col'), may hold values from -0.09375 to 0.09375
- source_feat: bfloat16 [16384, 256], P('row'), may hold values from -3.5 to 3.5
- target_feat: bfloat16 [4096, 256], P('col'), may hold values from -3.5 to 3.5
- source_type: int32 [16384], P('row'), may hold values from 0 to 15
- target_type: int32 [4096], P('col'), may hold values from 0 to 15
- row_weight: float32 [16384], P('row'), may hold values from 0.5 to 10
- col_weight: float32 [4096], P('col'), may hold values from 0.5 to 2
Outputs:
- coupling_next: bfloat16 [16384, 4096], P('row', 'col')
- barycentre: bfloat16 [16384, 256], P(('row', 'col'))
Inputs may be any that keep to these rules, and one draw needn't show every extreme that they name: `source_dist`: symmetric.
All inputs are finite; a program needn't handle non-finite values.
Results may differ from a plain program's by a relative error of at most 0.02.
Values may be sent and summed in bfloat16 or wider, within the bound.
A program may use at most 128 MiB of HBM per device.

v0:
```python
import math

import jax
import jax.numpy as jnp
from jax import lax
from jax.sharding import PartitionSpec as P

coupling_weight = 0.5
feature_weight = 2.5
mismatch_cost = 1.0


def from_everyone(value, axis):
    copies = jnp.broadcast_to(value, (lax.axis_size(axis), *value.shape))
    return lax.all_to_all(copies, axis, split_axis=0, concat_axis=0, tiled=True)


def all_in_one(value, axis):
    leaves = jax.tree.leaves(value)
    turns = sorted(range(len(leaves)), key=lambda k: -leaves[k].size)
    width = (1, *leaves[turns[0]].shape)[-1]
    lines = [
        jnp.pad(leaves[k].reshape(-1), (0, -leaves[k].size % width)).reshape(-1, width)
        for k in turns
    ]
    both, at, found = (from_everyone(jnp.concatenate(lines), axis), 0, {})
    for k, line in zip(turns, lines):
        share = both[:, at : at + len(line)].reshape(len(both), -1)
        found[k] = share[:, : leaves[k].size].reshape(-1, *leaves[k].shape)
        at += len(line)
    numbers = iter(range(len(leaves)))
    return jax.tree.map(lambda _: found[next(numbers)], value)


def combined_pairwise(pieces, combine):
    while len(jax.tree.leaves(pieces)[0]) > 1:
        pieces = jax.vmap(combine)(
            *(jax.tree.map(lambda part: part[side::2], pieces) for side in (0, 1))
        )
    return jax.tree.map(lambda part: part[0], pieces)


def combined_all(value, axis, combine):
    pieces = all_in_one(value, axis)
    return combined_pairwise(pieces, combine)


def gathered_by_type(value, axis):
    leaves, found = (jax.tree.leaves(value), {})
    for first, a in enumerate(leaves):
        if first not in found:
            alike = [k for k, b in enumerate(leaves) if b.dtype == a.dtype]
            got = (
                all_in_one([leaves[k] for k in alike], axis)
                if len(alike) > 1
                else [from_everyone(a, axis)]
            )
            for k, b in zip(alike, got):
                found[k] = b
    numbers = iter(range(len(leaves)))
    return jax.tree.map(lambda _: found[next(numbers)], value)


def combined_all_2(value, axis, combine):
    pieces = gathered_by_type(value, axis)
    return combined_pairwise(pieces, combine)


def split_up(value, dim, length):
    lengths = value.shape
    pieces = value.reshape(*lengths[:dim], length, lengths[dim] // length, *lengths[dim + 1 :])
    return jnp.moveaxis(pieces, dim, 0)


def summed_on_arrival(value, axis, dim):
    length = lax.axis_size(axis)
    pieces = lax.all_to_all(split_up(value, dim, length), axis, 0, 0, tiled=True)
    return jnp.sum(pieces.astype(jnp.float32), axis=0)


def combine_stats(earlier, later):
    highest = jnp.maximum(earlier[0], later[0])
    return (
        highest,
        earlier[1] * jnp.exp(earlier[0] - highest) + later[1] * jnp.exp(later[0] - highest),
    )


def shards(
    coupling,
    source_dist,
    target_dist,
    source_feat,
    target_feat,
    source_type,
    target_type,
    row_weight,
    col_weight,
):
    row_count, col_count = coupling.shape
    feat_width = source_feat.shape[1]
    total_rows = row_count * lax.axis_size("row")
    total_cols = col_count * lax.axis_size("col")
    target_block = lax.all_gather(target_dist, "row", axis=0, tiled=True)
    first = jnp.dot(
        source_dist,
        lax.all_gather(coupling, "row", axis=0, tiled=True),
        preferred_element_type=jnp.float32,
    )
    first_whole = lax.all_gather(first.astype(jnp.bfloat16), "col", axis=1, tiled=True)
    second = jnp.dot(first_whole, target_block, preferred_element_type=jnp.float32)
    affinity = lax.dot_general(
        source_feat, target_feat, (((1,), (1,)), ((), ())), preferred_element_type=jnp.float32
    )
    mismatch = (source_type[:, None] != target_type[None, :]).astype(jnp.float32)
    score = (
        jnp.log(coupling.astype(jnp.float32))
        + coupling_weight * second
        + feature_weight / math.sqrt(feat_width) * affinity
        - mismatch_cost * mismatch
    )
    local_top = jnp.max(score, axis=1)
    local_sum = jnp.sum(jnp.exp(score - local_top[:, None]), axis=1)
    row_top, row_sum = combined_all((local_top, local_sum), "col", combine_stats)
    row_lse = row_top + jnp.log(row_sum)
    first_log = score - row_lse[:, None] + jnp.log(row_weight)[:, None] + math.log(total_cols)
    local_col_top = jnp.max(first_log, axis=0)
    local_col_sum = jnp.sum(jnp.exp(first_log - local_col_top[None, :]), axis=0)
    col_top, col_sum = combined_all_2((local_col_top, local_col_sum), "row", combine_stats)
    col_lse = col_top + jnp.log(col_sum)
    next_float = jnp.exp(
        first_log - col_lse[None, :] + jnp.log(col_weight)[None, :] + math.log(total_rows)
    )
    coupling_next = next_float.astype(jnp.bfloat16)
    numer = jnp.dot(coupling_next, target_feat, preferred_element_type=jnp.float32)
    mass = jnp.sum(next_float, axis=1, keepdims=True)
    numer_home, mass_home = (
        summed_on_arrival(numer.astype(jnp.bfloat16), "col", 0),
        summed_on_arrival(mass.astype(jnp.bfloat16), "col", 0),
    )
    return (coupling_next, (numer_home / mass_home).astype(jnp.bfloat16))


def solution(mesh):
    in_specs = (
        P("row", "col"),
        P("row", None),
        P("row", "col"),
        P("row", None),
        P("col", None),
        P("row"),
        P("col"),
        P("row"),
        P("col"),
    )
    out_specs = (P("row", "col"), P(("row", "col"), None))
    return jax.shard_map(shards, mesh=mesh, in_specs=in_specs, out_specs=out_specs, check_vma=False)
```

profile of v0, /device:TPU:1, one launch (start us, length us, event | category | flops | bytes accessed | tf_op | source)
XLA Modules:
  0.0 335.4 jit_solution(761586258189664936)
XLA Ops:
  7.2 0.7 all-gather.4.cloned.1.call-update
  8.0 0.7 all-gather.8.cloned.1.call-update
  8.7 105.0 %all-gather.4.cloned.1.call-done = bf16[16384,512]{1,0:T(8,128)(2,1)} async-done(((bf16[512,512]{1,0:T(8,128)(2,1)}), bf16[16384,512]{1,0:T(8,128)(2,1)}) %all-gather.4.cloned.1.call-update) | async-done | bytes 16777232 | tf_op jit(solution)/shard_map/all_gather | solution.py:107
  113.8 17.9 %convolution_convert_fusion = bf16[512,512]{1,0:T(8,128)(2,1)} fusion(bf16[512,16384]{1,0:T(8,128)(2,1)} %param.10, bf16[16384,512]{1,0:T(8,128)(2,1)} %all-gather.4.cloned.1.call-done), kind=kOutput, calls=%fused_computation.5 | convolution fusion | flops 8590196736 | bytes 34078720 | tf_op jit(solution)/shard_map/dot_general | solution.py:105
  131.9 50.5 %all-gather.8.cloned.1.call-done = bf16[4096,512]{1,0:T(8,128)(2,1)} async-done(((bf16[128,512]{1,0:T(8,128)(2,1)}), bf16[4096,512]{1,0:T(8,128)(2,1)}) %all-gather.8.cloned.1.call-update) | async-done | bytes 4194320 | tf_op jit(solution)/shard_map/all_gather | solution.py:104
  182.4 83.7 %all-gather.6.cloned.1.call-done = bf16[512,4096]{1,0:T(8,128)(2,1)} async-done(((bf16[512,512]{1,0:T(8,128)(2,1)}), bf16[512,4096]{1,0:T(8,128)(2,1)}) %all-gather.6.cloned.1.call-update) | async-done | bytes 4194320 | tf_op jit(solution)/shard_map/all_gather | solution.py:110
  266.0 5.9 %fusion.2 = f32[512,512]{0,1:T(8,128)S(1)} fusion(bf16[512,4096]{1,0:T(8,128)(2,1)} %all-gather.6.cloned.1.call-done, bf16[4096,512]{1,0:T(8,128)(2,1)} %all-gather.8.cloned.1.call-done, bf16[512,512]{0,1:T(8,128)(2,1)S(1)} %copy.19), kind=kOutput, calls=%fused_computation.4 | convolution fusion | flops 2148270080 | bytes 9961472 | tf_op jit(solution)/shard_map/dot_general | solution.py:111
  272.0 0.4 fusion.12
  272.6 0.6 broadcast_in_dim.4
  273.2 3.4 %all-to-all-start = ((f32[8,2,512]{2,1,0:T(2,128)}), f32[8,2,512]{2,1,0:T(2,128)S(1)}, u32[]{:S(2)}, u32[]{:S(2)}) async-start(f32[8,2,512]{2,1,0:T(2,128)} %broadcast_in_dim.4), calls=%async_computation | async-start | bytes 65536 | tf_op jit(solution)/shard_map/all_to_all | solution.py:15
  276.6 6.6 %all-to-all-done = f32[8,2,512]{2,1,0:T(2,128)S(1)} async-done(((f32[8,2,512]{2,1,0:T(2,128)}), f32[8,2,512]{2,1,0:T(2,128)S(1)}, u32[]{:S(2)}, u32[]{:S(2)}) %all-to-all-start) | async-done | bytes 32800 | tf_op jit(solution)/shard_map/all_to_all | solution.py:15
  283.7 0.4 exponential_reduce_fusion
  284.1 0.7 broadcast_in_dim.5
  284.8 11.5 %all-to-all-start.1 = ((f32[32,2,512]{2,1,0:T(2,128)}), f32[32,2,512]{2,1,0:T(2,128)S(1)}, u32[]{:S(2)}, u32[]{:S(2)}) async-start(f32[32,2,512]{2,1,0:T(2,128)} %broadcast_in_dim.5), calls=%async_computation.1 | async-start | bytes 262144 | tf_op jit(solution)/shard_map/all_to_all | solution.py:15
  296.3 9.2 %all-to-all-done.1 = f32[32,2,512]{2,1,0:T(2,128)S(1)} async-done(((f32[32,2,512]{2,1,0:T(2,128)}), f32[32,2,512]{2,1,0:T(2,128)S(1)}, u32[]{:S(2)}, u32[]{:S(2)}) %all-to-all-start.1) | async-done | bytes 131104 | tf_op jit(solution)/shard_map/all_to_all | solution.py:15
  306.1 0.4 fusion.3
  306.5 0.7 convert_element_type.49
  307.2 3.3 all-to-all-start.3
  310.5 1.1 convolution_convert_fusion.1
  311.6 5.3 %all-to-all-done.3 = bf16[8,64,1]{1,2,0:T(2,128)(2,1)S(1)} async-done(((bf16[8,64,1]{1,2,0:T(2,128)(2,1)}), bf16[8,64,1]{1,2,0:T(2,128)(2,1)S(1)}, u32[]{:S(2)}, u32[]{:S(2)}) %all-to-all-start.3) | async-done | bytes 1056 | tf_op jit(solution)/shard_map/all_to_all | solution.py:77
  316.9 3.4 %all-to-all-start.2 = ((bf16[8,64,256]{2,1,0:T(8,128)(2,1)}), bf16[8,64,256]{2,1,0:T(8,128)(2,1)S(1)}, u32[]{:S(2)}, u32[]{:S(2)}) async-start(bf16[8,64,256]{2,1,0:T(8,128)(2,1)} %bitcast.8), calls=%async_computation.2 | async-start | bytes 524288 | tf_op jit(solution)/shard_map/all_to_all | solution.py:77
  320.3 1.0 copy.23
  321.4 6.8 %all-to-all-done.2 = bf16[8,64,256]{2,1,0:T(8,128)(2,1)S(1)} async-done(((bf16[8,64,256]{2,1,0:T(8,128)(2,1)}), bf16[8,64,256]{2,1,0:T(8,128)(2,1)S(1)}, u32[]{:S(2)}, u32[]{:S(2)}) %all-to-all-start.2) | async-done | bytes 262176 | tf_op jit(solution)/shard_map/all_to_all | solution.py:77
  328.2 0.7 divide_convert_fusion
  (64 shorter events, 1.7 us)
Async XLA Ops:
  7.2 264.8 %copy-start = (bf16[512,256]{1,0:T(8,128)(2,1)S(1)}, bf16[512,256]{1,0:T(8,128)(2,1)}, u32[]{:S(2)}) copy-start(bf16[512,256]{1,0:T(8,128)(2,1)} %param.13) | copy-start | bytes 786436
  7.2 106.6 %all-gather.4.cloned.1.call-start = ((), (), s32[]{:S(2)}) async-start(), calls=%async_computation.4 | async-start | bytes 17301504 | tf_op jit(solution)/shard_map/all_gather | solution.py:107
  7.9 174.5 %all-gather.8.cloned.1.call-start = ((), (), s32[]{:S(2)}) async-start(), calls=%async_computation.6 | async-start | bytes 4325376 | tf_op jit(solution)/shard_map/all_gather | solution.py:104
  8.7 123.0 %copy-start.1 = (bf16[512,512]{1,0:T(8,128)(2,1)S(1)}, bf16[512,512]{1,0:T(8,128)(2,1)}, u32[]{:S(2)}) copy-start(bf16[512,512]{1,0:T(8,128)(2,1)} %param.9) | copy-start | bytes 1572868
  8.7 257.4 %all-gather.6.cloned.1.call-start = ((), (), s32[]{:S(2)}) async-start(), calls=%async_computation.5 | async-start | bytes 4718592 | tf_op jit(solution)/shard_map/all_gather | solution.py:110
  131.6 140.3 %copy-start.2 = (bf16[512,256]{1,0:T(8,128)(2,1)S(1)}, bf16[512,256]{1,0:T(8,128)(2,1)}, u32[]{:S(2)}) copy-start(bf16[512,256]{1,0:T(8,128)(2,1)} %param.12) | copy-start | bytes 786436
  131.6 140.3 %copy-start.5 = (s32[512]{0:T(512)S(1)}, s32[512]{0:T(512)}, u32[]{:S(2)}) copy-start(s32[512]{0:T(512)} %param.15) | copy-start | bytes 6148
  131.6 140.3 %copy-start.6 = (s32[512]{0:T(512)S(1)}, s32[512]{0:T(512)}, u32[]{:S(2)}) copy-start(s32[512]{0:T(512)} %param.14) | copy-start | bytes 6148
  131.6 145.0 %copy-start.3 = (f32[512]{0:T(512)S(1)}, f32[512]{0:T(512)}, u32[]{:S(2)}) copy-start(f32[512]{0:T(512)} %param.16) | copy-start | bytes 6148
  131.6 164.7 %copy-start.4 = (f32[512]{0:T(512)S(1)}, f32[512]{0:T(512)}, u32[]{:S(2)}) copy-start(f32[512]{0:T(512)} %param.17) | copy-start | bytes 6148
  273.2 10.0 %all-to-all-start = ((f32[8,2,512]{2,1,0:T(2,128)}), f32[8,2,512]{2,1,0:T(2,128)S(1)}, u32[]{:S(2)}, u32[]{:S(2)}) async-start(f32[8,2,512]{2,1,0:T(2,128)} %broadcast_in_dim.4), calls=%async_computation | async-start | bytes 65536 | tf_op jit(solution)/shard_map/all_to_all | solution.py:15
  284.8 20.7 %all-to-all-start.1 = ((f32[32,2,512]{2,1,0:T(2,128)}), f32[32,2,512]{2,1,0:T(2,128)S(1)}, u32[]{:S(2)}, u32[]{:S(2)}) async-start(f32[32,2,512]{2,1,0:T(2,128)} %broadcast_in_dim.5), calls=%async_computation.1 | async-start | bytes 262144 | tf_op jit(solution)/shard_map/all_to_all | solution.py:15
  307.2 9.7 %all-to-all-start.3 = ((bf16[8,64,1]{1,2,0:T(2,128)(2,1)}), bf16[8,64,1]{1,2,0:T(2,128)(2,1)S(1)}, u32[]{:S(2)}, u32[]{:S(2)}) async-start(bf16[8,64,1]{1,2,0:T(2,128)(2,1)} %convert_element_type.49), calls=%async_computation.3 | async-start | bytes 8192 | tf_op jit(solution)/shard_map/all_to_all | solution.py:77
  316.9 11.2 %all-to-all-start.2 = ((bf16[8,64,256]{2,1,0:T(8,128)(2,1)}), bf16[8,64,256]{2,1,0:T(8,128)(2,1)S(1)}, u32[]{:S(2)}, u32[]{:S(2)}) async-start(bf16[8,64,256]{2,1,0:T(8,128)(2,1)} %bitcast.8), calls=%async_computation.2 | async-start | bytes 524288 | tf_op jit(solution)/shard_map/all_to_all | solution.py:77
Sparse Core Ops, SparseCore 0:
  9.8 103.8 all-gather.3
  115.6 66.7 all-gather.7
  185.4 80.5 all-gather.5
where the time goes:
time: 337 us; the launch traced here: 335 us
  waiting for transfers between devices  268 us (80%)
  matrix products  25.2 us (7%)
  starting transfers between devices  21.7 us (6%)
  between operations  14 us (4%)
  local copies, waits for them, and re-layouts  3.93 us (1%)
    all_gather x1, waiting for transfers between devices, shards(): lax.all_gather(coupling, 'row', axis=0, tiled=True)  105 us
    all_gather x1, waiting for transfers between devices, shards(): lax.all_gather(first.astype(jnp.bfloat16), 'col', axis=1, tiled=True)  83.7 us
    all_gather x1, waiting for transfers between devices, shards(): target_block = lax.all_gather(target_dist, 'row', axis=0, tiled=True)  50.5 us
    dot_general x1, matrix products, shards(): jnp.dot(source_dist, lax.all_gather(coupling, 'row', axis=0, tiled=True),...  17.9 us
    all_to_all x2, waiting for transfers between devices, from_everyone(): return lax.all_to_all(copies, axis, split_axis=0, concat_axis=0, tiled=True)  15.8 us
    all_to_all x2, starting transfers between devices, from_everyone(): return lax.all_to_all(copies, axis, split_axis=0, concat_axis=0, tiled=True)  14.9 us
    all_to_all x2, waiting for transfers between devices, summed_on_arrival(): lax.all_to_all(split_up(value, dim, length), axis, 0, 0, tiled=True)  12.1 us
  transfers between devices with their start and end apart: 7, of which 7 were waited for; matrix products, arithmetic and copies ran while one was open for 6% of the time, Pallas kernels for 0%

commit v1 on v0

v1 whole, which is shorter than its diff:
```python
import math

import jax
import jax.numpy as jnp
from jax import lax
from jax.experimental import pallas as pl
from jax.experimental.pallas import tpu as pltpu
from jax.sharding import PartitionSpec as P

MESH = pl.DeviceIdType.MESH
F32 = jnp.float32
BF16 = jnp.bfloat16

coupling_weight = 0.5
feature_weight = 2.5
mismatch_cost = 1.0

NZ = 8
NROW = 32
NCOL = 8
B = 512
H = B // 2
TB = 128
SB = B // NCOL
FEAT = 256
RT = 64
DIRS = (1, -1)
GROUPS = [(0, 0)] + [(s, d) for s in (1, 2, 3) for d in DIRS] + [(4, 1)]


def group_id(s, d):
    return GROUPS.index((s, {0: 0, 4: 1}.get(s, d)))


def lanes_to_tile(top, bottom):
    return jnp.concatenate(
        [v[:, k * 128 : (k + 1) * 128] for v in (top, bottom) for k in range(B // 128)], axis=0
    )


def tile_to_lanes(tile):
    return jnp.concatenate([tile[k : k + 1, :] for k in range(B // 128)], axis=1)


def to_sublanes(row):
    return jnp.transpose(jnp.broadcast_to(row, (128, B)))


def kernel(
    coupling,
    source_dist,
    target_dist,
    source_feat,
    target_feat,
    source_type,
    target_type,
    row_weight,
    col_weight,
    next_out,
    bary_out,
    dist,
    cbuf,
    tbuf,
    fbuf,
    acc,
    acc2,
    pre,
    sfeat,
    tfeat,
    stype,
    ttype,
    roww,
    colw,
    stat,
    rstat,
    cstat,
    nxt,
    parts,
    got,
    bary,
    in_sem,
    dist_sem,
    out_sem,
    zs_sem,
    zr_sem,
    ys_sem,
    yr_sem,
    bs_sem,
    br_sem,
    fs_sem,
    fr_sem,
    rs_sem,
    rr_sem,
    cs_sem,
    cr_sem,
    ps_sem,
    pr_sem,
):
    row = lax.axis_index("row")
    col = lax.axis_index("col")
    z = row // 4
    lane = (row // 2) % 2
    core = row % 2
    x = col % 4
    yhi = col // 4

    def row_at(zz, line):
        return zz * 4 + line * 2 + core

    def zpos(s, d):
        return (z + NZ - d * s) % NZ

    z_dev = {d: (((z + NZ + d) % NZ) * 4 + lane * 2 + core, col) for d in DIRS}
    y_dev = (z * 4 + (1 - lane) * 2 + core, col)
    sib_dev = (z * 4 + lane * 2 + 1 - core, col)
    x_dev = {d: (row, yhi * 4 + (x + 4 + d) % 4) for d in DIRS}
    hi_dev = (row, (1 - yhi) * 4 + x)

    own_in = []

    def bring(k, src, dst):
        copy = pltpu.make_async_copy(src, dst, in_sem.at[k])
        copy.start()
        own_in.append(copy)

    mine = pl.ds(pl.multiple_of(row * B, B), B)
    bring(0, coupling.at[:, pl.ds(0, H)], cbuf.at[0, mine])
    bring(1, coupling.at[:, pl.ds(H, H)], cbuf.at[1, mine])
    bring(2, target_dist, tbuf.at[pl.ds(pl.multiple_of(row * TB, TB), TB)])
    bring(3, source_feat, sfeat)
    bring(4, target_feat, tfeat)
    bring(5, source_type, stype)
    bring(6, target_type, ttype)
    bring(7, row_weight, roww)
    bring(8, col_weight, colw)

    def dist_copy(zz):
        span = pl.ds(pl.multiple_of(zz * 4 * B, 4 * B), 4 * B)
        return pltpu.make_async_copy(source_dist.at[:, span], dist.at[:, span], dist_sem.at[zz])

    for g, (s, d) in enumerate(GROUPS):
        dist_copy(zpos(s, d)).start()

    barrier = pltpu.get_barrier_semaphore()
    for j in range(1, NROW):
        pl.semaphore_signal(
            barrier, inc=1, device_id=((row + j) % NROW, col), device_id_type=MESH
        )
    for j in range(1, NCOL):
        pl.semaphore_signal(
            barrier, inc=1, device_id=(row, (col + j) % NCOL), device_id_type=MESH
        )
    pl.semaphore_wait(barrier, NROW - 1 + NCOL - 1)

    started = []

    def remote(src, dst, ssem, rsem, dev):
        return pltpu.make_async_remote_copy(
            src_ref=src,
            dst_ref=dst,
            send_sem=ssem,
            recv_sem=rsem,
            device_id=dev,
            device_id_type=MESH,
        )

    def send(copy):
        copy.start()
        started.append(copy)

    bufs = [cbuf.at[0], cbuf.at[1], tbuf]
    sizes = [B, B, TB]

    def piece(p, origin, part, quarter=None):
        half = sizes[p] // 2
        start = origin * sizes[p] + part * half
        if quarter is None:
            return bufs[p].at[pl.ds(pl.multiple_of(start, half), half)]
        return bufs[p].at[pl.ds(pl.multiple_of(start + quarter * (half // 2), half // 2), half // 2)]

    def whole(p, origin):
        return bufs[p].at[pl.ds(pl.multiple_of(origin * sizes[p], sizes[p]), sizes[p])]

    KIND = [(0, 0), (0, 1), (1, 1)]

    def z_copy(p, kind, s, d, origin_z):
        other, part = KIND[kind]
        line = 1 - lane if other else lane
        quarter = None if s < 4 else (0 if d == 1 else 1)
        ref = piece(p, row_at(origin_z, line), part, quarter)
        n = ((p * 3 + kind) * 2 + (0 if d == 1 else 1)) * 4 + s - 1
        return remote(ref, ref, zs_sem.at[n], zr_sem.at[n], z_dev[d])

    def y_send_copy(p, g, part, incoming):
        s, d = GROUPS[g]
        line = 1 - lane if incoming else lane
        ref = piece(p, row_at(zpos(s, d), line), part)
        n = p * 9 + (8 if part == 1 else g)
        return remote(ref, ref, ys_sem.at[n], yr_sem.at[n], y_dev)

    def sib_copy(p, g, other, incoming):
        s, d = GROUPS[g]
        line = 1 - lane if other else lane
        origin = zpos(s, d) * 4 + line * 2 + (1 - core if incoming else core)
        ref = whole(p, origin)
        n = (p * 8 + g) * 2 + other
        return remote(ref, ref, bs_sem.at[n], br_sem.at[n], sib_dev)

    def z_forward(p, kind, s, d):
        if s < 4:
            send(z_copy(p, kind, s + 1, d, zpos(s, d)))

    def phase_start(p):
        send(y_send_copy(p, 0, 1, False))
        for kind in (1, 0):
            for d in DIRS:
                send(z_copy(p, kind, 1, d, z))
        send(y_send_copy(p, 0, 0, False))
        send(sib_copy(p, 0, 0, False))

    def phase_other(p):
        y_send_copy(p, 0, 1, True).wait_recv()
        for d in DIRS:
            send(z_copy(p, 2, 1, d, z))

    def other_to_sib(p, s):
        for d in DIRS if s in (1, 2, 3) else (0,):
            g = group_id(s, d)
            y_send_copy(p, g, 0, True).wait_recv()
            send(sib_copy(p, g, 1, False))

    def phase_step(p, s):
        for d in DIRS:
            for kind in (1, 0):
                z_copy(p, kind, s, d, zpos(s, d)).wait_recv()
                z_forward(p, kind, s, d)
            if s < 4:
                send(y_send_copy(p, group_id(s, d), 0, False))
                send(sib_copy(p, group_id(s, d), 0, False))
        if s == 4:
            send(y_send_copy(p, group_id(4, 0), 0, False))
            send(sib_copy(p, group_id(4, 0), 0, False))
        for d in DIRS:
            z_copy(p, 2, s, d, zpos(s, d)).wait_recv()
            z_forward(p, 2, s, d)
        other_to_sib(p, s - 1)

    def sib_wait(p, g):
        for other in (0, 1):
            sib_copy(p, g, other, True).wait_recv()

    def groups_at(s):
        return [g for g, (t, _) in enumerate(GROUPS) if t == s]

    def matmul_first(p, s):
        for g in groups_at(s):
            sib_wait(p, g)
            zz = zpos(*GROUPS[g])
            if p == 0:
                dist_copy(zz).wait()

            def body(k, _):
                at = pl.multiple_of(zz * (4 * B) + k * B, B)
                prod = jnp.dot(
                    dist[:, pl.ds(at, B)], cbuf[p, pl.ds(at, B), :], preferred_element_type=F32
                )
                acc[...] += prod
                return 0

            lax.fori_loop(0, 4, body, 0)

    def first_copy(h, at_col, ssem_id, dev, span=None):
        ref = fbuf.at[at_col, h]
        if span is not None:
            ref = ref.at[pl.ds(span * H, H)]
        n = h * 9 + ssem_id
        return remote(ref, ref, fs_sem.at[n], fr_sem.at[n], dev)

    def x_col(y, s, d):
        return y * 4 + (x + 4 - d * s) % 4

    def x_copy(h, other, s, d, origin):
        n = 1 + other * 4 + (s - 1) * 2 + (0 if d == 1 else 1)
        span = None if s == 1 else (0 if d == 1 else 1)
        return first_copy(h, origin, n, x_dev[d], span)

    def gather_first_start(h):
        fbuf[col, h] = acc[...].astype(BF16)
        acc[...] = jnp.zeros_like(acc)
        send(first_copy(h, col, 0, hi_dev))
        for d in DIRS:
            send(x_copy(h, 0, 1, d, col))

    def gather_first_1(h):
        first_copy(h, (1 - yhi) * 4 + x, 0, hi_dev).wait_recv()
        for d in DIRS:
            send(x_copy(h, 1, 1, d, (1 - yhi) * 4 + x))
        for d in DIRS:
            x_copy(h, 0, 1, d, x_col(yhi, 1, d)).wait_recv()
            send(x_copy(h, 0, 2, d, x_col(yhi, 1, d)))

    def gather_first_2(h):
        for d in DIRS:
            x_copy(h, 1, 1, d, x_col(1 - yhi, 1, d)).wait_recv()
            send(x_copy(h, 1, 2, d, x_col(1 - yhi, 1, d)))

    def gather_first_3(h):
        for other in (0, 1):
            for d in DIRS:
                y = 1 - yhi if other else yhi
                x_copy(h, other, 2, d, x_col(y, 2, d)).wait_recv()

    def add_second(zz, h):
        at = pl.multiple_of(zz * B + h * H, H)
        acc2[...] += jnp.dot(fbuf[zz, h], tbuf[pl.ds(at, H), :], preferred_element_type=F32)

    def matmul_second(s):
        for g in groups_at(s):
            sib_wait(2, g)
            add_second(zpos(*GROUPS[g]), 0)

    def row_steps(body):
        lax.fori_loop(0, B // RT, lambda i, _: (body(pl.ds(pl.multiple_of(i * RT, RT), RT)), 0)[1], 0)

    def prepare():
        for copy in own_in[3:]:
            copy.wait()
        acc[...] = jnp.zeros_like(acc)
        acc2[...] = jnp.zeros_like(acc2)
        stat[...] = to_sublanes(stype[...].reshape(1, B).astype(F32))
        kinds = ttype[...].reshape(1, B).astype(F32)

        def body(rows):
            affinity = lax.dot_general(
                sfeat[rows, :], tfeat[...], (((1,), (1,)), ((), ())), preferred_element_type=F32
            )
            for h in range(2):
                base = pl.multiple_of(row * B + rows.start, RT)
                pre[rows, h * H : (h + 1) * H] = jnp.log(
                    cbuf[h, pl.ds(base, RT), :].astype(F32)
                )
            own = stat[rows, :]
            for k in range(B // 128):
                cut = slice(k * 128, (k + 1) * 128)
                mismatch = jnp.where(own != kinds[:, cut], 1.0, 0.0).astype(F32)
                pre[rows, cut] = (
                    pre[rows, cut]
                    + feature_weight / math.sqrt(FEAT) * affinity[:, cut]
                    - mismatch_cost * mismatch
                )

        row_steps(body)

    own_in[0].wait()
    phase_start(0)
    own_in[1].wait()
    own_in[2].wait()
    phase_other(0)
    prepare()
    phase_step(0, 1)
    phase_step(0, 2)
    matmul_first(0, 0)
    phase_step(0, 3)
    phase_start(1)
    matmul_first(0, 1)
    phase_step(0, 4)
    phase_other(1)
    matmul_first(0, 2)
    phase_step(1, 1)
    other_to_sib(0, 4)
    matmul_first(0, 3)
    phase_step(1, 2)
    matmul_first(0, 4)
    gather_first_start(0)
    matmul_first(1, 0)
    phase_step(1, 3)
    phase_start(2)
    gather_first_1(0)
    matmul_first(1, 1)
    phase_step(1, 4)
    phase_other(2)
    gather_first_2(0)
    matmul_first(1, 2)
    other_to_sib(1, 4)
    phase_step(2, 1)
    matmul_first(1, 3)
    matmul_first(1, 4)
    gather_first_start(1)
    phase_step(2, 2)
    gather_first_3(0)
    matmul_second(0)
    phase_step(2, 3)
    gather_first_1(1)
    matmul_second(1)
    phase_step(2, 4)
    gather_first_2(1)
    matmul_second(2)
    other_to_sib(2, 4)
    matmul_second(3)
    matmul_second(4)
    gather_first_3(1)
    lax.fori_loop(0, NCOL, lambda k, _: (add_second(k, 1), 0)[1], 0)

    spot = lax.broadcasted_iota(jnp.int32, (RT, 128), 1)

    def row_stats(rows):
        score = pre[rows, :] + coupling_weight * acc2[rows, :]
        pre[rows, :] = score
        top = jnp.max(score, axis=1, keepdims=True)
        total = jnp.sum(jnp.exp(score - top), axis=1, keepdims=True)
        stat[rows, :] = jnp.where(spot < 64, top, total)

    row_steps(row_stats)
    turned = jnp.transpose(stat[...])
    rstat[col] = lanes_to_tile(turned[0:1, :], turned[64:65, :])
    for j in range(1, NCOL):
        send(
            remote(
                rstat.at[col],
                rstat.at[col],
                rs_sem.at[j],
                rr_sem.at[j],
                (row, (col + j) % NCOL),
            )
        )
    for j in range(1, NCOL):
        came = (col + NCOL - j) % NCOL
        remote(rstat.at[came], rstat.at[came], rs_sem.at[j], rr_sem.at[j], (row, came)).wait_recv()

    def combined(ref):
        tops = ref[:, 0:4, :]
        top = jnp.max(tops, axis=0)
        total = jnp.sum(ref[:, 4:8, :] * jnp.exp(tops - top[None]), axis=0)
        return top + jnp.log(total)

    row_lse = tile_to_lanes(combined(rstat))
    shift = jnp.log(roww[...].reshape(1, B)) + math.log(NCOL * B) - row_lse
    stat[...] = to_sublanes(shift)

    def shifted(rows, best):
        move = stat[rows, :]
        tops = []
        for k in range(B // 128):
            cut = slice(k * 128, (k + 1) * 128)
            value = pre[rows, cut] + move
            pre[rows, cut] = value
            tops.append(jnp.max(value, axis=0, keepdims=True))
        return jnp.maximum(best, jnp.concatenate(tops, axis=1))

    def over_rows(body, start):
        return lax.fori_loop(
            0, B // RT, lambda i, c: body(pl.ds(pl.multiple_of(i * RT, RT), RT), c), start
        )

    col_top = over_rows(shifted, jnp.full((1, B), -jnp.inf, F32))
    col_sum = over_rows(
        lambda rows, c: c + jnp.sum(jnp.exp(pre[rows, :] - col_top), axis=0, keepdims=True),
        jnp.zeros((1, B), F32),
    )
    cstat[row] = lanes_to_tile(col_top, col_sum)
    for j in range(1, NROW):
        send(
            remote(
                cstat.at[row],
                cstat.at[row],
                cs_sem.at[j],
                cr_sem.at[j],
                ((row + j) % NROW, col),
            )
        )
    for j in range(1, NROW):
        came = (row + NROW - j) % NROW
        remote(cstat.at[came], cstat.at[came], cs_sem.at[j], cr_sem.at[j], (came, col)).wait_recv()
    col_shift = (
        jnp.log(colw[...].reshape(1, B)) + math.log(NROW * B) - tile_to_lanes(combined(cstat))
    )

    def finish(rows):
        value = jnp.exp(pre[rows, :] + col_shift)
        rounded = value.astype(BF16)
        nxt[rows, :] = rounded
        parts[rows, 0:FEAT] = jnp.dot(rounded, tfeat[...], preferred_element_type=F32).astype(BF16)
        mass = jnp.sum(value, axis=1, keepdims=True)
        high = mass.astype(BF16).astype(F32)
        parts[rows, FEAT : FEAT + 128] = jnp.where(spot < 64, high, mass - high).astype(BF16)

    row_steps(finish)
    out_copy = pltpu.make_async_copy(nxt, next_out, out_sem.at[0])
    out_copy.start()

    def part_of(c):
        return parts.at[pl.ds(pl.multiple_of(c * SB, SB), SB)]

    for j in range(1, NCOL):
        goes = (col + j) % NCOL
        send(remote(part_of(goes), got.at[col], ps_sem.at[j], pr_sem.at[j], (row, goes)))
    total = parts[pl.ds(pl.multiple_of(col * SB, SB), SB), :].astype(F32)
    for j in range(1, NCOL):
        came = (col + NCOL - j) % NCOL
        remote(part_of(came), got.at[came], ps_sem.at[j], pr_sem.at[j], (row, came)).wait_recv()
        total = total + got[came].astype(F32)
    mass = total[:, FEAT : FEAT + 1] + total[:, FEAT + 64 : FEAT + 65]
    bary[...] = (total[:, 0:FEAT] / mass).astype(BF16)
    bary_copy = pltpu.make_async_copy(bary, bary_out, out_sem.at[1])
    bary_copy.start()

    for copy in started:
        copy.wait_send()
    out_copy.wait()
    bary_copy.wait()


def shards(*args):
    anywhere = pl.BlockSpec(memory_space=pl.ANY)
    dma = pltpu.SemaphoreType.DMA
    return tuple(
        pl.pallas_call(
            kernel,
            out_shape=(
                jax.ShapeDtypeStruct((B, B), BF16),
                jax.ShapeDtypeStruct((SB, FEAT), BF16),
            ),
            in_specs=[anywhere] * 9,
            out_specs=(anywhere, anywhere),
            scratch_shapes=[
                pltpu.VMEM((B, NROW * B), BF16),
                pltpu.VMEM((2, NROW * B, H), BF16),
                pltpu.VMEM((NROW * TB, B), BF16),
                pltpu.VMEM((NCOL, 2, B, H), BF16),
                pltpu.VMEM((B, H), F32),
                pltpu.VMEM((B, B), F32),
                pltpu.VMEM((B, B), F32),
                pltpu.VMEM((B, FEAT), BF16),
                pltpu.VMEM((B, FEAT), BF16),
                pltpu.VMEM((B,), jnp.int32),
                pltpu.VMEM((B,), jnp.int32),
                pltpu.VMEM((B,), F32),
                pltpu.VMEM((B,), F32),
                pltpu.VMEM((B, 128), F32),
                pltpu.VMEM((NCOL, 8, 128), F32),
                pltpu.VMEM((NROW, 8, 128), F32),
                pltpu.VMEM((B, B), BF16),
                pltpu.VMEM((B, FEAT + 128), BF16),
                pltpu.VMEM((NCOL, SB, FEAT + 128), BF16),
                pltpu.VMEM((SB, FEAT), BF16),
                dma((9,)),
                dma((NZ,)),
                dma((2,)),
                dma((72,)),
                dma((72,)),
                dma((27,)),
                dma((27,)),
                dma((48,)),
                dma((48,)),
                dma((18,)),
                dma((18,)),
                dma((NCOL,)),
                dma((NCOL,)),
                dma((NROW,)),
                dma((NROW,)),
                dma((NCOL,)),
                dma((NCOL,)),
            ],
            compiler_params=pltpu.CompilerParams(
                collective_id=0, has_side_effects=True, vmem_limit_bytes=60 * 2**20
            ),
            name="mirror_step",
        )(*args)
    )


def solution(mesh):
    in_specs = (
        P("row", "col"),
        P("row", None),
        P("row", "col"),
        P("row", None),
        P("col", None),
        P("row"),
        P("col"),
        P("row"),
        P("col"),
    )
    out_specs = (P("row", "col"), P(("row", "col"), None))
    return jax.shard_map(shards, mesh=mesh, in_specs=in_specs, out_specs=out_specs, check_vma=False)
```

time: 337 us -> 142 us (0.42)
  waiting for transfers between devices: 268 us -> 0 us
  Pallas kernels: 0 us -> 138 us
  matrix products: 25.2 us -> 0 us
  starting transfers between devices: 21.7 us -> 0 us
  between operations: 14 us -> 0.64 us
    all_gather x3 -> x0, waiting for transfers between devices: 239 us -> none  [the longest x1 105 us: shards(): lax.all_gather(coupling, 'row', axis=0, tiled=True)]
    pallas_call x0 -> x1, Pallas kernels: none -> 138 us  [shards(): pl.pallas_call(kernel, out_shape=(jax.ShapeDtypeStruct((B, B), BF16), jax...]
    all_to_all x4 -> x0, waiting for transfers between devices: 27.9 us -> none  [the longest x2 15.8 us: from_everyone(): return lax.all_to_all(copies, axis, split_axis=0, concat_axis=0, tiled=True)]
    dot_general x4 -> x0, matrix products: 25.2 us -> none  [the longest x1 17.9 us: shards(): jnp.dot(source_dist, lax.all_gather(coupling, 'row', axis=0, tiled=True),...]
    all_to_all x4 -> x0, starting transfers between devices: 21.6 us -> none  [the longest x2 14.9 us: from_everyone(): return lax.all_to_all(copies, axis, split_axis=0, concat_axis=0, tiled=True)]
  transfers between devices with their start and end apart: 7 -> 0, of which waited for: 7 -> 0; matrix products, arithmetic and copies ran while one was open for 6% -> 0% of each run, Pallas kernels for 0% -> 0%
where the time goes in v1:
time: 142 us
  Pallas kernels  138 us (97%)
  local copies, waits for them, and re-layouts  3.24 us (2%)
    pallas_call x1, Pallas kernels, shards(): pl.pallas_call(kernel, out_shape=(jax.ShapeDtypeStruct((B, B), BF16), jax...  138 us
    unnamed x2, local copies, waits for them, and re-layouts  3.24 us

profile of v1, /device:TPU:1, one launch (start us, length us, event | category | flops | bytes accessed | tf_op | source)
XLA Modules:
  0.0 141.8 jit_solution(15890041411801901498)
XLA Ops:
  0.6 138.0 %mirror_step.1 = (bf16[512,512]{1,0:T(8,128)(2,1)}, bf16[64,256]{1,0:T(8,128)(2,1)}) custom-call(bf16[512,512]{1,0:T(8,128)(2,1)} %coupling.1, bf16[512,16384]{1,0:T(8,128)(2,1)} %source_dist.1, bf16[128,512]{1,0:T(8,128)(2,1)} %target_dist.1, bf16[512,256]{1,0:T(8,128)(2,1)} %source_feat.1, bf16[512,256]{1,0:T(8,128)(2,1)} %target_feat.1, s32[512]{0:T(512)} %source_type.1, ...), custom_call_target="tpu_custom_call" | custom-call | tf_op jit(solution)/shard_map/mirror_step/pallas_call | solution.py:517
  138.6 1.9 %copy.13 = bf16[512,512]{1,0:T(8,128)(2,1)} copy(bf16[512,512]{1,0:T(8,128)(2,1)} %get-tuple-element.4) | data formatting | bytes 1048576
  140.5 1.4 copy.14

commit v2 on v1

v2 whole, which is shorter than its diff:
```python
import functools
import math

import jax
import jax.numpy as jnp
from jax import lax
from jax.experimental import pallas as pl
from jax.experimental.pallas import tpu as pltpu
from jax.sharding import PartitionSpec as P

MESH = pl.DeviceIdType.MESH
F32 = jnp.float32
BF16 = jnp.bfloat16

coupling_weight = 0.5
feature_weight = 2.5
mismatch_cost = 1.0

NZ = 8
NROW = 32
NCOL = 8
B = 512
NP = 2
R = B // NP
Q = R // 4
TB = 128
SB = B // NCOL
FEAT = 256
RT = 64
DIRS = (1, -1)
GROUPS = [(0, 0)] + [(s, d) for s in (1, 2, 3) for d in DIRS] + [(4, 1)]


def group_id(s, d):
    return GROUPS.index((s, {0: 0, 4: 1}.get(s, d)))


def lanes_to_tile(top, bottom):
    return jnp.concatenate(
        [v[:, k * 128 : (k + 1) * 128] for v in (top, bottom) for k in range(B // 128)], axis=0
    )


def tile_to_lanes(tile):
    return jnp.concatenate([tile[k : k + 1, :] for k in range(B // 128)], axis=1)


def to_sublanes(row):
    return jnp.transpose(jnp.broadcast_to(row, (128, B)))


def kernel(
    coupling,
    source_dist,
    target_dist,
    source_feat,
    target_feat,
    source_type,
    target_type,
    row_weight,
    col_weight,
    next_hbm,
    bary_hbm,
    dist,
    tbuf,
    gbuf,
    fbuf,
    acc,
    second,
    pre,
    sfeat,
    tfeat,
    stype,
    ttype,
    roww,
    colw,
    stat,
    rstat,
    cstat,
    next_out,
    bary_out,
    parts,
    got,
    in_sem,
    dist_sem,
    out_sem,
    zs_sem,
    zr_sem,
    ys_sem,
    yr_sem,
    bs_sem,
    br_sem,
    fs_sem,
    fr_sem,
    rs_sem,
    rr_sem,
    cs_sem,
    cr_sem,
    ps_sem,
    pr_sem,
):
    row = lax.axis_index("row")
    col = lax.axis_index("col")
    z = row // 4
    lane = (row // 2) % 2
    core = row % 2
    x = col % 4
    yhi = col // 4

    def row_at(zz, line):
        return zz * 4 + line * 2 + core

    def zpos(s, d):
        return (z + NZ - d * s) % NZ

    z_dev = {d: (((z + NZ + d) % NZ) * 4 + lane * 2 + core, col) for d in DIRS}
    y_dev = (z * 4 + (1 - lane) * 2 + core, col)
    sib_dev = (z * 4 + lane * 2 + 1 - core, col)
    x_dev = {d: (row, yhi * 4 + (x + 4 + d) % 4) for d in DIRS}
    hi_dev = (row, (1 - yhi) * 4 + x)

    barrier = pltpu.get_barrier_semaphore()
    near = (*z_dev.values(), y_dev, sib_dev, *x_dev.values(), hi_dev)
    for dev in near:
        pl.semaphore_signal(barrier, inc=1, device_id=dev, device_id_type=MESH)
    own_in = []

    def bring(k, src, dst):
        copy = pltpu.make_async_copy(src, dst, in_sem.at[k])
        copy.start()
        own_in.append(copy)

    for m in range(NP):
        bring(m, coupling.at[pl.ds(m * R, R)], fbuf.at[m, col])
    own_rows = pl.ds(pl.multiple_of(row * TB, TB), TB)
    bring(NP, target_dist, tbuf.at[own_rows])
    bring(3, source_feat, sfeat)
    bring(4, target_feat, tfeat)
    bring(5, source_type, stype)
    bring(6, target_type, ttype)
    bring(7, row_weight, roww)
    bring(8, col_weight, colw)

    def dist_copy(m, zz, k):
        origin = zz * 4 + k
        src = pl.ds(pl.multiple_of(origin * B + m * R, R), R)
        dst = pl.ds(pl.multiple_of(origin * R, R), R)
        return pltpu.make_async_copy(
            source_dist.at[:, src], dist.at[m, :, dst], dist_sem.at[m * NROW + origin]
        )

    pl.semaphore_wait(barrier, len(near))

    started = []

    def remote(src, dst, ssem, rsem, dev):
        return pltpu.make_async_remote_copy(
            src_ref=src,
            dst_ref=dst,
            send_sem=ssem,
            recv_sem=rsem,
            device_id=dev,
            device_id_type=MESH,
        )

    def send(copy):
        copy.start()
        started.append(copy)

    bufs = [tbuf] + [gbuf.at[m] for m in range(NP)]
    sizes = [TB] + [R] * NP

    def piece(p, origin, part, quarter=None):
        half = sizes[p] // 2
        start = origin * sizes[p] + part * half
        if quarter is None:
            return bufs[p].at[pl.ds(pl.multiple_of(start, half), half)]
        return bufs[p].at[pl.ds(pl.multiple_of(start + quarter * (half // 2), half // 2), half // 2)]

    def whole(p, origin):
        return bufs[p].at[pl.ds(pl.multiple_of(origin * sizes[p], sizes[p]), sizes[p])]

    KIND = [(0, 0), (0, 1), (1, 1)]

    def z_copy(p, kind, s, d, origin_z):
        other, part = KIND[kind]
        line = 1 - lane if other else lane
        quarter = None if s < 4 else (0 if d == 1 else 1)
        ref = piece(p, row_at(origin_z, line), part, quarter)
        n = ((p * 3 + kind) * 2 + (0 if d == 1 else 1)) * 4 + s - 1
        return remote(ref, ref, zs_sem.at[n], zr_sem.at[n], z_dev[d])

    def y_send_copy(p, g, part, incoming):
        s, d = GROUPS[g]
        line = 1 - lane if incoming else lane
        ref = piece(p, row_at(zpos(s, d), line), part)
        n = p * 9 + (8 if part == 1 else g)
        return remote(ref, ref, ys_sem.at[n], yr_sem.at[n], y_dev)

    def sib_copy(p, g, other, incoming):
        s, d = GROUPS[g]
        line = 1 - lane if other else lane
        origin = zpos(s, d) * 4 + line * 2 + (1 - core if incoming else core)
        ref = whole(p, origin)
        n = (p * 8 + g) * 2 + other
        return remote(ref, ref, bs_sem.at[n], br_sem.at[n], sib_dev)

    def z_forward(p, kind, s, d):
        if s < 4:
            send(z_copy(p, kind, s + 1, d, zpos(s, d)))

    def phase_start(ps, then=lambda: None):
        for p in ps:
            send(y_send_copy(p, 0, 1, False))
        then()
        for kind in (0, 1):
            for p in ps:
                for d in DIRS:
                    send(z_copy(p, kind, 1, d, z))
        for p in ps:
            send(y_send_copy(p, 0, 0, False))
            send(sib_copy(p, 0, 0, False))

    def phase_other(ps):
        for p in ps:
            y_send_copy(p, 0, 1, True).wait_recv()
            for d in DIRS:
                send(z_copy(p, 2, 1, d, z))

    def other_to_sib(ps, s):
        for p in ps:
            for d in DIRS if s in (1, 2, 3) else (0,):
                g = group_id(s, d)
                y_send_copy(p, g, 0, True).wait_recv()
                send(sib_copy(p, g, 1, False))

    work = []

    def do_some(count=1):
        for _ in range(min(count, len(work))):
            work.pop(0)()

    def do_all():
        do_some(len(work))

    def phase_step(ps, s, count=1):
        for kind in (0, 1, 2):
            for p in ps:
                for d in DIRS:
                    z_copy(p, kind, s, d, zpos(s, d)).wait_recv()
                    z_forward(p, kind, s, d)
                    if kind == 0 and s < 4:
                        send(y_send_copy(p, group_id(s, d), 0, False))
                    if kind == 1 and s < 4:
                        send(sib_copy(p, group_id(s, d), 0, False))
                    do_some(count)
                if kind == 0 and s == 4:
                    send(y_send_copy(p, group_id(4, 0), 0, False))
                if kind == 1 and s == 4:
                    send(sib_copy(p, group_id(4, 0), 0, False))
        other_to_sib(ps, s - 1)

    def sib_wait(p, g):
        for other in (0, 1):
            sib_copy(p, g, other, True).wait_recv()

    def groups_at(s):
        return [g for g, (t, _) in enumerate(GROUPS) if t == s]

    def matmul_piece(p, g, at):
        m = p - 1
        zz = zpos(*GROUPS[g])
        if at == 0:
            sib_wait(p, g)
            for k in range(4):
                dist_copy(m, zz, k).wait()
        rows = pl.ds(pl.multiple_of(zz * (4 * R) + at * B, B), B)
        second[...] += jnp.dot(dist[m, :, rows], gbuf[m, rows, :], preferred_element_type=F32)

    def matmul(p, s):
        for g in groups_at(s):
            for at in range(4 * R // B):
                work.append(functools.partial(matmul_piece, p, g, at))

    def first_copy(m, n, at_col, dev, start, size):
        ref = fbuf.at[m, at_col, pl.ds(start, size)]
        n = m * 22 + n
        return remote(ref, ref, fs_sem.at[n], fr_sem.at[n], dev)

    def x_col(other, s, d):
        y = 1 - yhi if other else yhi
        return y * 4 + (x + 4 - d * s) % 4

    def way(d):
        return 0 if d == 1 else 1

    hi_col = (1 - yhi) * 4 + x

    def hi_copy(m, q, at_col):
        return first_copy(m, q, at_col, hi_dev, q * Q, Q)

    def own_copy(m, s, d, at_col):
        n = 4 + (s - 1) * 2 + way(d)
        if s == 1:
            return first_copy(m, n, at_col, x_dev[d], 0, R)
        return first_copy(m, n, at_col, x_dev[d], way(d) * 2 * Q, 2 * Q)

    def other_copy(m, q, s, d, at_col):
        n = 8 + q * 2 + way(d) if s == 1 else 16 + q
        return first_copy(m, n, at_col, x_dev[d], q * Q, Q)

    def hi_send(m, q):
        send(hi_copy(m, q, col))

    def own_send(m):
        for d in DIRS:
            send(own_copy(m, 1, d, col))

    def own_pass(m):
        for d in DIRS:
            own_copy(m, 1, d, x_col(0, 1, d)).wait_recv()
            send(own_copy(m, 2, d, x_col(0, 1, d)))

    def own_end(m):
        for d in DIRS:
            own_copy(m, 2, d, x_col(0, 2, d)).wait_recv()

    def hi_pass(m, q):
        hi_copy(m, q, hi_col).wait_recv()
        for d in DIRS:
            send(other_copy(m, q, 1, d, hi_col))

    def other_pass(m, q):
        for d in DIRS:
            other_copy(m, q, 1, d, x_col(1, 1, d)).wait_recv()
        d = 1 if q < 2 else -1
        send(other_copy(m, q, 2, d, x_col(1, 1, d)))

    def other_end(m):
        for q in range(4):
            d = 1 if q < 2 else -1
            other_copy(m, q, 2, d, x_col(1, 2, d)).wait_recv()

    def multiply(m, c):
        rows = pl.ds(pl.multiple_of(c * B, B), B)
        acc[m] += jnp.dot(fbuf[m, c], tbuf[rows, :], preferred_element_type=F32)

    def multiply_group(m, g):
        sib_wait(0, g)
        multiply(m, zpos(*GROUPS[g]))

    def keep(m):
        piece_rows = pl.ds(pl.multiple_of(row * R, R), R)
        gbuf[m, piece_rows, :] = acc[m].astype(BF16)

    def build_line(m, other, steps):
        base = (1 - yhi if other else yhi) * 4
        for k in steps:
            work.append(functools.partial(multiply, m, base + (x + k) % 4))

    def build_groups(m, s):
        for g in groups_at(s):
            work.append(functools.partial(multiply_group, m, g))

    def prepare_start():
        for copy in own_in[NP + 1 :]:
            copy.wait()
        stat[...] = to_sublanes(stype[...].reshape(1, B).astype(F32))

    def prepare(m, at):
        kinds = ttype[...].reshape(1, B).astype(F32)
        rows = pl.ds(m * R + at, RT)
        affinity = lax.dot_general(
            sfeat[rows, :], tfeat[...], (((1,), (1,)), ((), ())), preferred_element_type=F32
        )
        base = jnp.log(fbuf[m, col, pl.ds(at, RT), :].astype(F32))
        own = stat[rows, :]
        for k in range(B // 128):
            cut = slice(k * 128, (k + 1) * 128)
            mismatch = jnp.where(own != kinds[:, cut], 1.0, 0.0).astype(F32)
            pre[rows, cut] = (
                base[:, cut]
                + feature_weight / math.sqrt(FEAT) * affinity[:, cut]
                - mismatch_cost * mismatch
            )

    later = functools.partial
    td, g0, g1 = ((p,) for p in range(3))
    own_in[0].wait()
    own_in[NP].wait()
    phase_start(td, later(hi_send, 0, 0))
    own_send(0)
    for m in range(NP):
        for s, d in GROUPS:
            for k in range(4):
                dist_copy(m, zpos(s, d), k).start()
    for ref in (acc, second):
        ref[...] = jnp.zeros_like(ref)
    phase_other(td)
    hi_send(0, 1)
    work.append(later(own_pass, 0))
    work.append(later(hi_pass, 0, 0))
    phase_step(td, 1)
    hi_send(0, 2)
    work.append(later(hi_pass, 0, 1))
    work.append(later(other_pass, 0, 0))
    phase_step(td, 2)
    hi_send(0, 3)
    work.append(later(hi_pass, 0, 2))
    work.append(later(other_pass, 0, 1))
    work.append(later(own_end, 0))
    phase_step(td, 3)
    work.append(later(hi_pass, 0, 3))
    work.append(later(other_pass, 0, 2))
    phase_step(td, 4)
    do_all()
    other_to_sib(td, 4)
    own_in[1].wait()
    other_pass(0, 3)
    hi_send(1, 0)
    own_send(1)
    other_end(0)
    for s in range(5):
        build_groups(0, s)
    work.append(later(keep, 0))
    do_all()
    phase_start(g0)
    hi_send(1, 1)
    prepare_start()
    for at in range(0, R, RT):
        work.append(later(prepare, 0, at))
    phase_other(g0)
    hi_send(1, 2)
    own_pass(1)
    hi_pass(1, 0)
    work.append(later(hi_pass, 1, 1))
    for at in range(0, R, RT):
        work.append(later(prepare, 1, at))
    phase_step(g0, 1)
    hi_send(1, 3)
    work.append(later(other_pass, 1, 0))
    work.append(later(hi_pass, 1, 2))
    work.append(later(own_end, 1))
    build_line(1, 0, range(4))
    phase_step(g0, 2, 2)
    work.append(later(other_pass, 1, 1))
    work.append(later(hi_pass, 1, 3))
    work.append(later(other_pass, 1, 2))
    build_line(1, 1, (0,))
    work.append(later(other_pass, 1, 3))
    build_line(1, 1, (1, 3))
    phase_step(g0, 3, 2)
    do_all()
    other_end(1)
    build_line(1, 1, (2,))
    work.append(later(keep, 1))
    do_all()
    phase_start(g1)
    matmul(1, 0)
    matmul(1, 1)
    phase_step(g0, 4)
    do_all()
    phase_other(g1)
    matmul(1, 2)
    work.insert(2, later(other_to_sib, g0, 4))
    phase_step(g1, 1)
    matmul(1, 3)
    matmul(1, 4)
    phase_step(g1, 2, 2)
    matmul(2, 0)
    phase_step(g1, 3, 2)
    matmul(2, 1)
    phase_step(g1, 4)
    do_some(2)
    other_to_sib(g1, 4)
    matmul(2, 2)
    matmul(2, 3)
    matmul(2, 4)
    do_all()

    def row_steps(body):
        lax.fori_loop(0, B // RT, lambda i, _: (body(pl.ds(pl.multiple_of(i * RT, RT), RT)), 0)[1], 0)

    spot = lax.broadcasted_iota(jnp.int32, (RT, 128), 1)

    def row_stats(rows):
        score = pre[rows, :] + coupling_weight * second[rows, :]
        pre[rows, :] = score
        top = jnp.max(score, axis=1, keepdims=True)
        total = jnp.sum(jnp.exp(score - top), axis=1, keepdims=True)
        stat[rows, :] = jnp.where(spot < 64, top, total)

    row_steps(row_stats)
    turned = jnp.transpose(stat[...])
    rstat[col] = lanes_to_tile(turned[0:1, :], turned[64:65, :])
    for j in range(1, NCOL):
        send(
            remote(
                rstat.at[col],
                rstat.at[col],
                rs_sem.at[j],
                rr_sem.at[j],
                (row, (col + j) % NCOL),
            )
        )
    for j in range(1, NCOL):
        came = (col + NCOL - j) % NCOL
        remote(rstat.at[came], rstat.at[came], rs_sem.at[j], rr_sem.at[j], (row, came)).wait_recv()

    def combined(ref):
        tops = ref[:, 0:4, :]
        top = jnp.max(tops, axis=0)
        total = jnp.sum(ref[:, 4:8, :] * jnp.exp(tops - top[None]), axis=0)
        return top + jnp.log(total)

    row_lse = tile_to_lanes(combined(rstat))
    shift = jnp.log(roww[...].reshape(1, B)) + math.log(NCOL * B) - row_lse
    stat[...] = to_sublanes(shift)

    def shifted(rows, best):
        move = stat[rows, :]
        tops = []
        for k in range(B // 128):
            cut = slice(k * 128, (k + 1) * 128)
            value = pre[rows, cut] + move
            pre[rows, cut] = value
            tops.append(jnp.max(value, axis=0, keepdims=True))
        return jnp.maximum(best, jnp.concatenate(tops, axis=1))

    def over_rows(body, start):
        return lax.fori_loop(
            0, B // RT, lambda i, c: body(pl.ds(pl.multiple_of(i * RT, RT), RT), c), start
        )

    col_top = over_rows(shifted, jnp.full((1, B), -jnp.inf, F32))
    col_sum = over_rows(
        lambda rows, c: c + jnp.sum(jnp.exp(pre[rows, :] - col_top), axis=0, keepdims=True),
        jnp.zeros((1, B), F32),
    )
    cstat[row] = lanes_to_tile(col_top, col_sum)
    for j in range(1, NROW):
        send(
            remote(
                cstat.at[row],
                cstat.at[row],
                cs_sem.at[j],
                cr_sem.at[j],
                ((row + j) % NROW, col),
            )
        )
    for j in range(1, NROW):
        came = (row + NROW - j) % NROW
        remote(cstat.at[came], cstat.at[came], cs_sem.at[j], cr_sem.at[j], (came, col)).wait_recv()
    col_shift = (
        jnp.log(colw[...].reshape(1, B)) + math.log(NROW * B) - tile_to_lanes(combined(cstat))
    )

    def part_of(c):
        return parts.at[pl.ds(pl.multiple_of(c * SB, SB), SB)]

    for j in (6, 2, 5, 7, 4, 3, 1, 0):
        goes = (col + j) % NCOL
        rows = pl.ds(pl.multiple_of(goes * SB, SB), SB)
        value = jnp.exp(pre[rows, :] + col_shift)
        rounded = value.astype(BF16)
        next_out[rows, :] = rounded
        parts[rows, 0:FEAT] = jnp.dot(rounded, tfeat[...], preferred_element_type=F32).astype(BF16)
        mass = jnp.sum(value, axis=1, keepdims=True)
        high = mass.astype(BF16).astype(F32)
        parts[rows, FEAT : FEAT + 128] = jnp.where(spot < 64, high, mass - high).astype(BF16)
        if j:
            send(remote(part_of(goes), got.at[col], ps_sem.at[j], pr_sem.at[j], (row, goes)))
    out_copy = pltpu.make_async_copy(next_out, next_hbm, out_sem.at[0])
    out_copy.start()

    total = parts[pl.ds(pl.multiple_of(col * SB, SB), SB), :].astype(F32)
    for j in range(1, NCOL):
        came = (col + NCOL - j) % NCOL
        remote(part_of(came), got.at[came], ps_sem.at[j], pr_sem.at[j], (row, came)).wait_recv()
        total = total + got[came].astype(F32)
    mass = total[:, FEAT : FEAT + 1] + total[:, FEAT + 64 : FEAT + 65]
    bary_out[...] = (total[:, 0:FEAT] / mass).astype(BF16)
    bary_copy = pltpu.make_async_copy(bary_out, bary_hbm, out_sem.at[1])
    bary_copy.start()

    for copy in started:
        copy.wait_send()
    out_copy.wait()
    bary_copy.wait()


def hand_over(next_in, bary_in, next_out, bary_out, sem):
    copies = (
        pltpu.make_async_copy(next_in, next_out, sem.at[0]),
        pltpu.make_async_copy(bary_in, bary_out, sem.at[1]),
    )
    for copy in copies:
        copy.start()
    for copy in copies:
        copy.wait()


def shards(*args):
    anywhere = pl.BlockSpec(memory_space=pl.ANY)
    dma = pltpu.SemaphoreType.DMA
    results = (
        pl.pallas_call(
            kernel,
            out_shape=(
                jax.ShapeDtypeStruct((B, B), BF16),
                jax.ShapeDtypeStruct((SB, FEAT), BF16),
            ),
            in_specs=[anywhere] * 9,
            out_specs=(anywhere, anywhere),
            scratch_shapes=[
                pltpu.VMEM((NP, B, NROW * R), BF16),
                pltpu.VMEM((NROW * TB, B), BF16),
                pltpu.VMEM((NP, NROW * R, B), BF16),
                pltpu.VMEM((NP, NCOL, R, B), BF16),
                pltpu.VMEM((NP, R, B), F32),
                pltpu.VMEM((B, B), F32),
                pltpu.VMEM((B, B), F32),
                pltpu.VMEM((B, FEAT), BF16),
                pltpu.VMEM((B, FEAT), BF16),
                pltpu.VMEM((B,), jnp.int32),
                pltpu.VMEM((B,), jnp.int32),
                pltpu.VMEM((B,), F32),
                pltpu.VMEM((B,), F32),
                pltpu.VMEM((B, 128), F32),
                pltpu.VMEM((NCOL, 8, 128), F32),
                pltpu.VMEM((NROW, 8, 128), F32),
                pltpu.VMEM((B, B), BF16),
                pltpu.VMEM((SB, FEAT), BF16),
                pltpu.VMEM((B, FEAT + 128), BF16),
                pltpu.VMEM((NCOL, SB, FEAT + 128), BF16),
                dma((NP + 7,)),
                dma((NP * NROW,)),
                dma((2,)),
                dma((72,)),
                dma((72,)),
                dma((27,)),
                dma((27,)),
                dma((48,)),
                dma((48,)),
                dma((44,)),
                dma((44,)),
                dma((NCOL,)),
                dma((NCOL,)),
                dma((NROW,)),
                dma((NROW,)),
                dma((NCOL,)),
                dma((NCOL,)),
            ],
            compiler_params=pltpu.CompilerParams(
                collective_id=0, has_side_effects=True, vmem_limit_bytes=60 * 2**20
            ),
            name="mirror_step",
        )(*args)
    )
    return tuple(
        pl.pallas_call(
            hand_over,
            out_shape=tuple(jax.ShapeDtypeStruct(r.shape, r.dtype) for r in results),
            in_specs=[pl.BlockSpec(memory_space=pltpu.VMEM)] * 2,
            out_specs=(anywhere, anywhere),
            scratch_shapes=[dma((2,))],
            name="hand_over",
        )(*results)
    )


def solution(mesh):
    in_specs = (
        P("row", "col"),
        P("row", None),
        P("row", "col"),
        P("row", None),
        P("col", None),
        P("row"),
        P("col"),
        P("row"),
        P("col"),
    )
    out_specs = (P("row", "col"), P(("row", "col"), None))
    return jax.shard_map(shards, mesh=mesh, in_specs=in_specs, out_specs=out_specs, check_vma=False)
```

time: 142 us -> 133 us (0.937)
  Pallas kernels: 138 us -> 132 us
  local copies, waits for them, and re-layouts: 3.24 us -> 0 us
    pallas_call x1, Pallas kernels: 138 us -> 130 us  [shards(): pl.pallas_call(kernel, out_shape=(jax.ShapeDtypeStruct((B, B), BF16), jax...]
    unnamed x2 -> x0, local copies, waits for them, and re-layouts: 3.24 us -> none
    pallas_call x0 -> x1, Pallas kernels: none -> 1.86 us  [shards(): pl.pallas_call(hand_over, out_shape=tuple((jax.ShapeDtypeStruct(r.shape,...]
where the time goes in v2:
time: 133 us
  Pallas kernels  132 us (99%)
    pallas_call x1, Pallas kernels, shards(): pl.pallas_call(kernel, out_shape=(jax.ShapeDtypeStruct((B, B), BF16), jax...  130 us

profile of v2, /device:TPU:1, one launch (start us, length us, event | category | flops | bytes accessed | tf_op | source)
XLA Modules:
  0.0 132.9 jit_solution(7586928821428430139)
XLA Ops:
  0.6 130.4 %mirror_step.1 = (bf16[512,512]{1,0:T(8,128)(2,1)}, bf16[64,256]{1,0:T(8,128)(2,1)}) custom-call(bf16[512,512]{1,0:T(8,128)(2,1)} %coupling.1, bf16[512,16384]{1,0:T(8,128)(2,1)} %source_dist.1, bf16[128,512]{1,0:T(8,128)(2,1)} %target_dist.1, bf16[512,256]{1,0:T(8,128)(2,1)} %source_feat.1, bf16[512,256]{1,0:T(8,128)(2,1)} %target_feat.1, s32[512]{0:T(512)} %source_type.1, ...), custom_call_target="tpu_custom_call" | custom-call | tf_op jit(solution)/shard_map/mirror_step/pallas_call | solution.py:607
  131.0 1.9 %hand_over.1 = (bf16[512,512]{1,0:T(8,128)(2,1)}, bf16[64,256]{1,0:T(8,128)(2,1)}) custom-call(bf16[512,512]{1,0:T(8,128)(2,1)} %get-tuple-element.4.next_in, bf16[64,256]{1,0:T(8,128)(2,1)} %get-tuple-element.5.bary_in), custom_call_target="tpu_custom_call" | custom-call | tf_op jit(solution)/shard_map/hand_over/pallas_call | solution.py:661

commit v3 on v2

--- a/solution.py
+++ b/solution.py
@@ -27,6 +27,7 @@
 SB = B // NCOL
 FEAT = 256
 RT = 64
+RS = 128
 DIRS = (1, -1)
 GROUPS = [(0, 0)] + [(s, d) for s in (1, 2, 3) for d in DIRS] + [(4, 1)]
 
@@ -169,13 +170,15 @@
 
     bufs = [tbuf] + [gbuf.at[m] for m in range(NP)]
     sizes = [TB] + [R] * NP
+    fronts = [TB // 4] + [R // 2] * NP
 
     def piece(p, origin, part, quarter=None):
-        half = sizes[p] // 2
-        start = origin * sizes[p] + part * half
-        if quarter is None:
-            return bufs[p].at[pl.ds(pl.multiple_of(start, half), half)]
-        return bufs[p].at[pl.ds(pl.multiple_of(start + quarter * (half // 2), half // 2), half // 2)]
+        size = sizes[p] - fronts[p] if part else fronts[p]
+        start = origin * sizes[p] + part * fronts[p]
+        if quarter is not None:
+            size //= 2
+            start = start + quarter * size
+        return bufs[p].at[pl.ds(pl.multiple_of(start, 16), size)]
 
     def whole(p, origin):
         return bufs[p].at[pl.ds(pl.multiple_of(origin * sizes[p], sizes[p]), sizes[p])]
@@ -389,6 +392,7 @@
     own_in[0].wait()
     own_in[NP].wait()
     phase_start(td, later(hi_send, 0, 0))
+    hi_send(0, 1)
     own_send(0)
     for m in range(NP):
         for s, d in GROUPS:
@@ -397,35 +401,35 @@
     for ref in (acc, second):
         ref[...] = jnp.zeros_like(ref)
     phase_other(td)
-    hi_send(0, 1)
-    work.append(later(own_pass, 0))
-    work.append(later(hi_pass, 0, 0))
+    hi_send(0, 2)
+    hi_send(0, 3)
+    own_in[1].wait()
+
+    def nothing():
+        pass
+
+    work += [nothing, nothing, later(own_pass, 0), later(hi_pass, 0, 0), later(hi_pass, 0, 1)]
     phase_step(td, 1)
-    hi_send(0, 2)
-    work.append(later(hi_pass, 0, 1))
-    work.append(later(other_pass, 0, 0))
+    do_all()
+    work += [nothing, later(hi_pass, 0, 2), nothing, nothing, later(hi_pass, 0, 3)]
     phase_step(td, 2)
-    hi_send(0, 3)
-    work.append(later(hi_pass, 0, 2))
-    work.append(later(other_pass, 0, 1))
-    work.append(later(own_end, 0))
+    do_all()
+    hi_send(1, 0)
+    work += [nothing, later(other_pass, 0, 0), later(other_pass, 0, 1), nothing, later(other_pass, 0, 2)]
     phase_step(td, 3)
-    work.append(later(hi_pass, 0, 3))
-    work.append(later(other_pass, 0, 2))
+    do_all()
+    work += [nothing, later(other_pass, 0, 3)]
     phase_step(td, 4)
-    do_all()
+    hi_send(1, 1)
+    own_send(1)
     other_to_sib(td, 4)
-    own_in[1].wait()
-    other_pass(0, 3)
-    hi_send(1, 0)
-    own_send(1)
+    own_end(0)
     other_end(0)
     for s in range(5):
         build_groups(0, s)
     work.append(later(keep, 0))
     do_all()
     phase_start(g0)
-    hi_send(1, 1)
     prepare_start()
     for at in range(0, R, RT):
         work.append(later(prepare, 0, at))
@@ -470,16 +474,16 @@
     matmul(2, 0)
     phase_step(g1, 3, 2)
     matmul(2, 1)
-    phase_step(g1, 4)
+    matmul(2, 2)
+    phase_step(g1, 4, 2)
+    matmul(2, 3)
     do_some(2)
     other_to_sib(g1, 4)
-    matmul(2, 2)
-    matmul(2, 3)
     matmul(2, 4)
     do_all()
 
     def row_steps(body):
-        lax.fori_loop(0, B // RT, lambda i, _: (body(pl.ds(pl.multiple_of(i * RT, RT), RT)), 0)[1], 0)
+        lax.fori_loop(0, B // RS, lambda i, _: (body(pl.ds(pl.multiple_of(i * RS, RS), RS)), 0)[1], 0)
 
     spot = lax.broadcasted_iota(jnp.int32, (RT, 128), 1)
 
@@ -488,7 +492,9 @@
         pre[rows, :] = score
         top = jnp.max(score, axis=1, keepdims=True)
         total = jnp.sum(jnp.exp(score - top), axis=1, keepdims=True)
-        stat[rows, :] = jnp.where(spot < 64, top, total)
+        stat[rows, :] = jnp.where(
+            lax.broadcasted_iota(jnp.int32, (RS, 128), 1) < 64, top, total
+        )
 
     row_steps(row_stats)
     turned = jnp.transpose(stat[...])
@@ -529,7 +535,7 @@
 
     def over_rows(body, start):
         return lax.fori_loop(
-            0, B // RT, lambda i, c: body(pl.ds(pl.multiple_of(i * RT, RT), RT), c), start
+            0, B // RS, lambda i, c: body(pl.ds(pl.multiple_of(i * RS, RS), RS), c), start
         )
 
     col_top = over_rows(shifted, jnp.full((1, B), -jnp.inf, F32))

time: 133 us -> 130 us (0.977)
  Pallas kernels: 132 us -> 129 us
    pallas_call x1, Pallas kernels: 130 us -> 127 us  [shards(): pl.pallas_call(kernel, out_shape=(jax.ShapeDtypeStruct((B, B), BF16), jax...]
where the time goes in v3:
time: 130 us
  Pallas kernels  129 us (99%)
    pallas_call x1, Pallas kernels, shards(): pl.pallas_call(kernel, out_shape=(jax.ShapeDtypeStruct((B, B), BF16), jax...  127 us

profile of v3, /device:TPU:1, one launch (start us, length us, event | category | flops | bytes accessed | tf_op | source)
XLA Modules:
  0.0 129.8 jit_solution(3368157047794958736)
XLA Ops:
  0.6 127.3 %mirror_step.1 = (bf16[512,512]{1,0:T(8,128)(2,1)}, bf16[64,256]{1,0:T(8,128)(2,1)}) custom-call(bf16[512,512]{1,0:T(8,128)(2,1)} %coupling.1, bf16[512,16384]{1,0:T(8,128)(2,1)} %source_dist.1, bf16[128,512]{1,0:T(8,128)(2,1)} %target_dist.1, bf16[512,256]{1,0:T(8,128)(2,1)} %source_feat.1, bf16[512,256]{1,0:T(8,128)(2,1)} %target_feat.1, s32[512]{0:T(512)} %source_type.1, ...), custom_call_target="tpu_custom_call" | custom-call | tf_op jit(solution)/shard_map/mirror_step/pallas_call | solution.py:613
  127.9 1.9 %hand_over.1 = (bf16[512,512]{1,0:T(8,128)(2,1)}, bf16[64,256]{1,0:T(8,128)(2,1)}) custom-call(bf16[512,512]{1,0:T(8,128)(2,1)} %get-tuple-element.4.next_in, bf16[64,256]{1,0:T(8,128)(2,1)} %get-tuple-element.5.bary_in), custom_call_target="tpu_custom_call" | custom-call | tf_op jit(solution)/shard_map/hand_over/pallas_call | solution.py:667

commit v4 on v3

--- a/solution.py
+++ b/solution.py
@@ -430,25 +430,25 @@
     work.append(later(keep, 0))
     do_all()
     phase_start(g0)
+    hi_send(1, 2)
     prepare_start()
     for at in range(0, R, RT):
         work.append(later(prepare, 0, at))
     phase_other(g0)
-    hi_send(1, 2)
+    hi_send(1, 3)
     own_pass(1)
     hi_pass(1, 0)
     work.append(later(hi_pass, 1, 1))
     for at in range(0, R, RT):
         work.append(later(prepare, 1, at))
     phase_step(g0, 1)
-    hi_send(1, 3)
     work.append(later(other_pass, 1, 0))
     work.append(later(hi_pass, 1, 2))
     work.append(later(own_end, 1))
+    work.append(later(other_pass, 1, 1))
+    work.append(later(hi_pass, 1, 3))
     build_line(1, 0, range(4))
     phase_step(g0, 2, 2)
-    work.append(later(other_pass, 1, 1))
-    work.append(later(hi_pass, 1, 3))
     work.append(later(other_pass, 1, 2))
     build_line(1, 1, (0,))
     work.append(later(other_pass, 1, 3))

time: 130 us -> 130 us (level)
  no operation moved by 1% of the time
where the time goes in v4:
time: 130 us
  Pallas kernels  129 us (99%)
    pallas_call x1, Pallas kernels, shards(): pl.pallas_call(kernel, out_shape=(jax.ShapeDtypeStruct((B, B), BF16), jax...  127 us

profile of v4, /device:TPU:1, one launch (start us, length us, event | category | flops | bytes accessed | tf_op | source)
XLA Modules:
  0.0 129.6 jit_solution(14588030669631375781)
XLA Ops:
  0.6 127.1 %mirror_step.1 = (bf16[512,512]{1,0:T(8,128)(2,1)}, bf16[64,256]{1,0:T(8,128)(2,1)}) custom-call(bf16[512,512]{1,0:T(8,128)(2,1)} %coupling.1, bf16[512,16384]{1,0:T(8,128)(2,1)} %source_dist.1, bf16[128,512]{1,0:T(8,128)(2,1)} %target_dist.1, bf16[512,256]{1,0:T(8,128)(2,1)} %source_feat.1, bf16[512,256]{1,0:T(8,128)(2,1)} %target_feat.1, s32[512]{0:T(512)} %source_type.1, ...), custom_call_target="tpu_custom_call" | custom-call | tf_op jit(solution)/shard_map/mirror_step/pallas_call | solution.py:613
  127.8 1.9 %hand_over.1 = (bf16[512,512]{1,0:T(8,128)(2,1)}, bf16[64,256]{1,0:T(8,128)(2,1)}) custom-call(bf16[512,512]{1,0:T(8,128)(2,1)} %get-tuple-element.4.next_in, bf16[64,256]{1,0:T(8,128)(2,1)} %get-tuple-element.5.bary_in), custom_call_target="tpu_custom_call" | custom-call | tf_op jit(solution)/shard_map/hand_over/pallas_call | solution.py:667
